TPU v7x, 32 devices: a whole 2x2x4 slice. The times are simulated.
32 devices in a mesh: group: 2 (over x), shard: 16 (over z, y, core).
Axes of the slice: x: 2, y: 2, z: 4, core: 2. Of those that a mesh axis runs over, the one named last changes fastest.
Arguments:
- rollout_rows: bfloat16 [512, 8192], P('group', 'shard'), may hold values from -6 to 6
- assign: int32 [512], replicated, may hold values from 0 to 511, each once
- cotangent: bfloat16 [512, 8192], P('group', 'shard'), may hold values from -3 to 3
- w_master: float32 [8192, 8192], P('group', 'shard'), may hold values from -0.0625 to 0.0625
- adam_m: float32 [8192, 8192], P('group', 'shard'), may hold values from -6 to 6
- adam_v: float32 [8192, 8192], P('group', 'shard'), may hold values from 0.05 to 1
- tile_mask: int32 [64, 64], replicated, may hold values from 0 to 1, as said below
Outputs:
- projected: bfloat16 [512, 8192], P('group', 'shard')
- input_grad: bfloat16 [512, 8192], P('group', 'shard')
- w_updated: float32 [8192, 8192], P('group', 'shard')
- m_updated: float32 [8192, 8192], P('group', 'shard')
- v_updated: float32 [8192, 8192], P('group', 'shard')
- rollout_tiles: bfloat16 [64, 6, 128, 128], P('shard')
Inputs may be any that keep to these rules, and one draw needn't show every extreme that they name: `tile_mask`: each tile column has 1 to 6 trainable tiles, and some column has exactly 6. `assign`: a permutation of the 512 rollout rows.
All inputs are finite; a program needn't handle non-finite values.
Results may differ from a plain program's by a relative error of at most 0.0051.
Values may be sent and summed in bfloat16 or wider, within the bound.
No kernel may reach another device: no remote copies, remote signals or barrier semaphores. Data moves between devices by JAX's collectives and lax.ppermute only.
A program may use at most 192 MiB of HBM per device.

v0:
```python
import jax
import jax.numpy as jnp
from jax import lax
from jax.sharding import PartitionSpec as P

TILE = 128
CAP = 6
beta_one = 0.9
beta_two = 0.999
learn_rate = 0.02
eps_adam = 1e-08
bias_one = 1.0 - 0.9**10
bias_two = 1.0 - 0.999**10


def shards(rollout_rows, assign, cotangent, w_master, adam_m, adam_v, tile_mask):
    group_at = lax.axis_index("group")
    shard_at = lax.axis_index("shard")
    row_count = cotangent.shape[0]
    col_tiles = cotangent.shape[1] // TILE
    row_tiles = w_master.shape[0] // TILE
    w_half = w_master.astype(jnp.bfloat16)
    all_rows, w_cols = (
        lax.all_gather(rollout_rows, "group", axis=0, tiled=True),
        lax.all_gather(w_half, "group", axis=0, tiled=True),
    )
    my_rows = lax.dynamic_slice_in_dim(assign, group_at * row_count, row_count)
    picked = jnp.take(all_rows, my_rows, axis=0)
    x_full, dy_full = (
        lax.all_gather(picked, "shard", axis=1, tiled=True),
        lax.all_gather(cotangent, "shard", axis=1, tiled=True),
    )
    projected = jnp.dot(x_full, w_cols, preferred_element_type=jnp.float32).astype(jnp.bfloat16)
    w_rows = lax.all_to_all(w_cols, "shard", split_axis=0, concat_axis=1, tiled=True)
    input_grad = lax.dot_general(
        dy_full, w_rows, (((1,), (1,)), ((), ())), preferred_element_type=jnp.float32
    ).astype(jnp.bfloat16)
    mask_cols = lax.dynamic_slice_in_dim(tile_mask, shard_at * col_tiles, col_tiles, 1)
    row_order = jnp.argsort(1 - mask_cols, axis=0, stable=True)
    slot_index = row_order[:CAP].T
    counts = jnp.sum(mask_cols, axis=0)
    live_slot = jnp.arange(CAP)[None, :] < counts[:, None]
    owner_rows = group_at * row_tiles + jnp.arange(row_tiles)
    owner_map = (
        (slot_index[:, :, None] == owner_rows[None, None, :]) & live_slot[:, :, None]
    ).astype(jnp.float32)
    partial_value = lax.dot_general(
        x_full, cotangent, (((0,), (0,)), ((), ())), preferred_element_type=jnp.float32
    )
    gradient = lax.psum_scatter(
        partial_value.astype(jnp.bfloat16), "group", scatter_dimension=0, tiled=True
    ).astype(jnp.float32)
    mask_local = (
        lax.dynamic_slice(
            tile_mask, (group_at * row_tiles, shard_at * col_tiles), (row_tiles, col_tiles)
        )
        > 0
    )
    mask_wide = jnp.broadcast_to(
        mask_local[:, None, :, None], (row_tiles, TILE, col_tiles, TILE)
    ).reshape(w_master.shape)
    m_updated = jnp.where(mask_wide, beta_one * adam_m + (1.0 - beta_one) * gradient, adam_m)
    v_updated = jnp.where(
        mask_wide, beta_two * adam_v + (1.0 - beta_two) * gradient * gradient, adam_v
    )
    adam_step = m_updated / bias_one / (jnp.sqrt(v_updated / bias_two) + eps_adam)
    w_updated = jnp.where(mask_wide, w_master - learn_rate * adam_step, w_master)
    new_tiles = w_updated.reshape(row_tiles, TILE, col_tiles, TILE).transpose(0, 2, 1, 3)
    fresh_terms = jnp.einsum(
        "cjk,kcab->cjab", owner_map, new_tiles, precision=lax.Precision.HIGHEST
    )
    rollout_tiles = lax.psum(fresh_terms.astype(jnp.bfloat16), "group")
    return (projected, input_grad, w_updated, m_updated, v_updated, rollout_tiles)


def solution(mesh):
    placed = (
        P("group", "shard"),
        P(),
        P("group", "shard"),
        P("group", "shard"),
        P("group", "shard"),
        P("group", "shard"),
        P(),
    )
    return jax.shard_map(
        shards,
        mesh=mesh,
        in_specs=placed,
        out_specs=(
            P("group", "shard"),
            P("group", "shard"),
            P("group", "shard"),
            P("group", "shard"),
            P("group", "shard"),
            P("shard", None, None, None),
        ),
        check_vma=False,
    )
```

profile of v0, /device:TPU:13, one launch (start us, length us, event | category | flops | bytes accessed | tf_op | source)
XLA Modules:
  0.0 546.4 jit_solution(14071634290224153602)
XLA Ops:
  7.2 0.0 all-gather.4.cloned.1.call-start
  7.2 0.8 compare_and_fusion
  8.0 8.1 %all_gather.12 = bf16[512,512]{1,0:T(8,128)(2,1)S(1)} all-gather(bf16[256,512]{1,0:T(8,128)(2,1)} %param.7), channel_id=1, replica_groups=mesh['group'=2,'shard'=16] {'group'}, dimensions={0}, use_global_device_ids=true | all-gather | bytes 786432 | tf_op jit(solution)/shard_map/all_gather | solution.py:24
  16.1 1.2 gather_fusion
  17.2 0.8 broadcast_select_fusion
  18.0 0.0 all-gather.4.cloned.1.call-update
  18.0 0.0 copy-start
  18.1 0.0 reduce-scatter.2.cloned.1.call-start
  18.1 52.3 %all-gather.4.cloned.1.call-done = bf16[256,8192]{1,0:T(8,128)(2,1)} async-done(((bf16[256,512]{1,0:T(8,128)(2,1)}), bf16[256,8192]{1,0:T(8,128)(2,1)}) %all-gather.4.cloned.1.call-update) | async-done | bytes 4194320 | tf_op jit(solution)/shard_map/all_gather | solution.py:30
  70.4 8.0 %convolution_convert_fusion = bf16[8192,512]{1,0:T(8,128)(2,1)} fusion(bf16[256,8192]{1,0:T(8,128)(2,1)} %all-gather.4.cloned.1.call-done, bf16[256,512]{1,0:T(8,128)(2,1)} %param.9), kind=kOutput, calls=%fused_computation.3 | convolution fusion | flops 2151677952 | bytes 12845056 | tf_op jit(solution)/shard_map/dot_general | solution.py:47
  78.4 0.0 reduce-scatter.2.cloned.1.call-update
  78.5 0.0 all-gather.6.cloned.1.call-start
  78.5 0.0 copy-done
  78.5 0.1 dynamic-slice_compare_fusion
  78.6 99.5 %reduce-scatter.2.cloned.1.call-done = bf16[4096,512]{1,0:T(8,128)(2,1)} async-done(((bf16[8192,512]{1,0:T(8,128)(2,1)}), bf16[4096,512]{1,0:T(8,128)(2,1)}) %reduce-scatter.2.cloned.1.call-update) | async-done | bytes 4194320 | tf_op jit(solution)/shard_map/reduce_scatter | solution.py:50
  178.1 1.1 broadcast_in_dim.26
  179.3 22.2 %subtract_select_fusion = (f32[4096,512]{1,0:T(8,128)}, f32[4096,512]{1,0:T(8,128)}, f32[4096,512]{1,0:T(8,128)}, bf16[4096,512]{1,0:T(8,128)(2,1)}) fusion(f32[4096,512]{1,0:T(8,128)} %param.10, pred[512,8,4,128]{3,2,1,0:T(4,128)(4,1)S(1)} %bitcast.31, f32[4096,512]{1,0:T(8,128)} %param.11, bf16[4096,512]{1,0:T(8,128)(2,1)} %reduce-scatter.2.cloned.1.call-done, ...), kind=kLoop, calls=%fused_computation.1 | loop fusion | flops 37748736 | bytes 60817408 | tf_op jit(solution)/shard_map/jit(_where)/select_n | solution.py:67
  201.5 0.0 all-gather.6.cloned.1.call-update
  201.5 104.2 %all-gather.6.cloned.1.call-done = bf16[8192,512]{1,0:T(8,128)(2,1)} async-done(((bf16[4096,512]{1,0:T(8,128)(2,1)}), bf16[8192,512]{1,0:T(8,128)(2,1)}) %all-gather.6.cloned.1.call-update) | async-done | bytes 8388624 | tf_op jit(solution)/shard_map/all_gather | solution.py:25
  305.6 6.5 %all-to-all-start = ((bf16[16,512,512]{2,1,0:T(8,128)(2,1)}), bf16[16,512,512]{2,1,0:T(8,128)(2,1)}, u32[]{:S(2)}, u32[]{:S(2)}) async-start(bf16[16,512,512]{2,1,0:T(8,128)(2,1)} %bitcast.29), calls=%async_computation | async-start | bytes 16777216 | tf_op jit(solution)/shard_map/all_to_all | solution.py:34
  312.1 0.2 all-reduce.2.cloned.1.call-start
  312.4 0.1 dynamic-slice_reduce_fusion
  312.5 1.0 sort.17
  313.5 0.1 copy.19
  313.6 0.1 iota_compare_fusion
  313.7 9.9 %reshape.54 = f32[32,128,4,128]{3,2,1,0:T(4,128)} reshape(f32[4096,512]{1,0:T(8,128)} %get-tuple-element.26) | data formatting | bytes 16777216 | tf_op jit(solution)/shard_map/reshape | solution.py:68
  323.6 11.6 %fusion.7 = bf16[4,6,128,128]{3,1,2,0:T(8,128)(2,1)} fusion(f32[32,128,4,128]{3,2,1,0:T(4,128)} %reshape.54, s32[32]{0:T(128)S(1)} %iota_add_fusion, s32[4,6]{1,0:T(4,128)S(1)} %copy.19, pred[4,6]{1,0:T(4,128)(4,1)S(1)} %iota_compare_fusion), kind=kOutput, calls=%fused_computation.12 | convolution fusion | flops 151389696 | bytes 9175288 | tf_op jit(solution)/shard_map/cjk,kcab->cjab/dot_general | solution.py:69
  335.1 0.0 all-reduce.2.cloned.1.call-update
  335.2 0.0 all-gather.8.cloned.1.call-start
  335.2 0.5 all-gather.8.cloned.1.call-update
  335.8 39.2 %all-reduce.2.cloned.1.call-done = bf16[4,6,128,128]{3,1,2,0:T(8,128)(2,1)} async-done(((bf16[4,6,128,128]{3,1,2,0:T(8,128)(2,1)}), bf16[4,6,128,128]{3,1,2,0:T(8,128)(2,1)}) %all-reduce.2.cloned.1.call-update) | async-done | bytes 786448 | tf_op jit(solution)/shard_map/psum | solution.py:72
  374.9 2.3 copy.21
  377.2 7.7 %convolution_convert_fusion.2 = bf16[256,512]{1,0:T(8,128)(2,1)} fusion(bf16[256,8192]{1,0:T(8,128)(2,1)} %all-gather.4.cloned.1.call-done, bf16[8192,512]{1,0:T(8,128)(2,1)} %all-gather.6.cloned.1.call-done), kind=kOutput, calls=%fused_computation.14 | convolution fusion | flops 2147614720 | bytes 12845056 | tf_op jit(solution)/shard_map/dot_general | solution.py:33
  384.9 135.0 %all-to-all-done = bf16[16,512,512]{2,1,0:T(8,128)(2,1)} async-done(((bf16[16,512,512]{2,1,0:T(8,128)(2,1)}), bf16[16,512,512]{2,1,0:T(8,128)(2,1)}, u32[]{:S(2)}, u32[]{:S(2)}) %all-to-all-start) | async-done | bytes 8388640 | tf_op jit(solution)/shard_map/all_to_all | solution.py:34
  519.9 12.3 %copy.18 = bf16[512,16,512]{0,2,1:T(8,128)(2,1)} copy(bf16[512,16,512]{2,0,1:T(8,128)(2,1)} %bitcast.1) | data formatting | bytes 16777216 | tf_op jit(solution)/shard_map/all_to_all | solution.py:34
  532.2 0.0 all-gather.8.cloned.1.call-done
  532.2 7.7 %convolution_convert_fusion.1 = bf16[256,512]{1,0:T(8,128)(2,1)} fusion(bf16[256,8192]{1,0:T(8,128)(2,1)} %all-gather.8.cloned.1.call-done, bf16[512,8192]{0,1:T(8,128)(2,1)} %bitcast.30), kind=kOutput, calls=%fused_computation.13 | convolution fusion | flops 2147614720 | bytes 12845056 | tf_op jit(solution)/shard_map/dot_general | solution.py:35
  (4 shorter events, 0.0 us)
Async XLA Ops:
  7.2 63.3 %all-gather.4.cloned.1.call-start = ((), (), s32[]{:S(2)}) async-start(), calls=%async_computation.2 | async-start | bytes 4456448 | tf_op jit(solution)/shard_map/all_gather | solution.py:30
  18.0 60.5 %copy-start = (s32[64,64]{1,0:T(8,128)S(1)}, s32[64,64]{1,0:T(8,128)}, u32[]{:S(2)}) copy-start(s32[64,64]{1,0:T(8,128)} %param.13) | copy-start | bytes 49156
  18.1 160.1 %reduce-scatter.2.cloned.1.call-start = ((), (), s32[]{:S(2)}) async-start(), calls=%async_computation.5 | async-start | bytes 12582912 | tf_op jit(solution)/shard_map/reduce_scatter | solution.py:50
  78.5 227.2 %all-gather.6.cloned.1.call-start = ((), (), s32[]{:S(2)}) async-start(), calls=%async_computation.3 | async-start | bytes 12582912 | tf_op jit(solution)/shard_map/all_gather | solution.py:25
  305.6 214.2 %all-to-all-start = ((bf16[16,512,512]{2,1,0:T(8,128)(2,1)}), bf16[16,512,512]{2,1,0:T(8,128)(2,1)}, u32[]{:S(2)}, u32[]{:S(2)}) async-start(bf16[16,512,512]{2,1,0:T(8,128)(2,1)} %bitcast.29), calls=%async_computation | async-start | bytes 16777216 | tf_op jit(solution)/shard_map/all_to_all | solution.py:34
  312.1 62.8 %all-reduce.2.cloned.1.call-start = ((), (), s32[]{:S(2)}) async-start(), calls=%async_computation.6 | async-start | bytes 2097152 | tf_op jit(solution)/shard_map/psum | solution.py:72
  335.2 197.0 %all-gather.8.cloned.1.call-start = ((), (), s32[]{:S(2)}) async-start(), calls=%async_computation.4 | async-start | bytes 4456448 | tf_op jit(solution)/shard_map/all_gather | solution.py:31
Sparse Core Ops, SparseCore 0:
  18.2 52.2 all-gather.3
  78.6 99.5 reduce-scatter.1
  201.6 103.9 all-gather.5
  335.3 39.5 all-reduce.1
  376.9 115.9 all-gather.7
where the time goes:
time: 547 us; the launch traced here: 546 us
  waiting for transfers between devices  431 us (79%)
  matrix products  34.9 us (6%)
  local copies, waits for them, and re-layouts  26.9 us (5%)
  other arithmetic  25 us (5%)
  between operations  13.8 us (3%)
  blocking collectives  8.06 us (1%)
  starting transfers between devices  6.89 us (1%)
    all_to_all x1, waiting for transfers between devices, shards(): lax.all_to_all(w_cols, 'shard', split_axis=0, concat_axis=1, tiled=True)  135 us
    all_gather x1, waiting for transfers between devices, shards(): lax.all_gather(w_half, 'group', axis=0, tiled=True)  104 us
    reduce_scatter x1, waiting for transfers between devices, shards(): lax.psum_scatter(partial_value.astype(jnp.bfloat16), 'group', scatter_dim...  99.5 us
    all_gather x1, waiting for transfers between devices, shards(): lax.all_gather(picked, 'shard', axis=1, tiled=True)  52.3 us
    psum x1, waiting for transfers between devices, shards(): rollout_tiles = lax.psum(fresh_terms.astype(jnp.bfloat16), 'group')  39.2 us
    select_n x1, other arithmetic, shards(): jnp.where(mask_wide, w_master - learn_rate * adam_step, w_master)  22.2 us
    all_to_all x1, local copies, waits for them, and re-layouts, shards(): lax.all_to_all(w_cols, 'shard', split_axis=0, concat_axis=1, tiled=True)  12.3 us
    dot_general x1, matrix products, shards(): jnp.einsum('cjk,kcab->cjab', owner_map, new_tiles, precision=lax.Precisio...  11.6 us
  transfers between devices with their start and end apart: 6, of which 5 were waited for; matrix products, arithmetic and copies ran while one was open for 8% of the time, Pallas kernels for 0%

commit v1 on v0

--- a/solution.py
+++ b/solution.py
@@ -31,7 +31,10 @@
         lax.all_gather(cotangent, "shard", axis=1, tiled=True),
     )
     projected = jnp.dot(x_full, w_cols, preferred_element_type=jnp.float32).astype(jnp.bfloat16)
-    w_rows = lax.all_to_all(w_cols, "shard", split_axis=0, concat_axis=1, tiled=True)
+    size = lax.axis_size("shard")
+    blocks = jnp.stack(jnp.split(w_cols, size, axis=0), axis=0)
+    blocks = lax.all_to_all(blocks, "shard", split_axis=0, concat_axis=0)
+    w_rows = jnp.concatenate(blocks, axis=1)
     input_grad = lax.dot_general(
         dy_full, w_rows, (((1,), (1,)), ((), ())), preferred_element_type=jnp.float32
     ).astype(jnp.bfloat16)

time: 547 us -> 449 us (0.82)
  waiting for transfers between devices: 431 us -> 305 us
  local copies, waits for them, and re-layouts: 26.9 us -> 53 us
    all_to_all x1, waiting for transfers between devices: 135 us -> 26.9 us  [shards(): blocks = lax.all_to_all(blocks, 'shard', split_axis=0, concat_axis=0)]
    all_gather x1, waiting for transfers between devices: 0.01 us -> 70.7 us  [shards(): lax.all_gather(cotangent, 'shard', axis=1, tiled=True)]
    reduce_scatter x1, waiting for transfers between devices: 99.5 us -> 55.3 us  [shards(): lax.psum_scatter(partial_value.astype(jnp.bfloat16), 'group', scatter_dim...]
    unnamed x3 -> x22, local copies, waits for them, and re-layouts: 2.28 us -> 38.7 us
    psum x1, waiting for transfers between devices: 39.2 us -> 7.91 us  [shards(): rollout_tiles = lax.psum(fresh_terms.astype(jnp.bfloat16), 'group')]
    all_to_all x1 -> x0, local copies, waits for them, and re-layouts: 12.3 us -> none  [shards(): lax.all_to_all(w_cols, 'shard', split_axis=0, concat_axis=1, tiled=True)]
    all_gather x1, waiting for transfers between devices: 52.3 us -> 45 us  [shards(): lax.all_gather(picked, 'shard', axis=1, tiled=True)]
    all_gather x1, waiting for transfers between devices: 104 us -> 98.4 us  [shards(): lax.all_gather(w_half, 'group', axis=0, tiled=True)]
  transfers between devices with their start and end apart: 6 -> 6, of which waited for: 5 -> 6; matrix products, arithmetic and copies ran while one was open for 8% -> 24% of each run, Pallas kernels for 0% -> 0%
where the time goes in v1:
time: 449 us; the launch traced here: 446 us
  waiting for transfers between devices  305 us (68%)
  local copies, waits for them, and re-layouts  53 us (12%)
  matrix products  34.9 us (8%)
  other arithmetic  24.8 us (6%)
  between operations  13.8 us (3%)
  blocking collectives  8.06 us (2%)
  starting transfers between devices  6.85 us (2%)
    all_gather x1, waiting for transfers between devices, shards(): lax.all_gather(w_half, 'group', axis=0, tiled=True)  98.4 us
    all_gather x1, waiting for transfers between devices, shards(): lax.all_gather(cotangent, 'shard', axis=1, tiled=True)  70.7 us
    reduce_scatter x1, waiting for transfers between devices, shards(): lax.psum_scatter(partial_value.astype(jnp.bfloat16), 'group', scatter_dim...  55.3 us
    all_gather x1, waiting for transfers between devices, shards(): lax.all_gather(picked, 'shard', axis=1, tiled=True)  45 us
    unnamed x22, local copies, waits for them, and re-layouts  38.7 us
    all_to_all x1, waiting for transfers between devices, shards(): blocks = lax.all_to_all(blocks, 'shard', split_axis=0, concat_axis=0)  26.9 us
    select_n x1, other arithmetic, shards(): jnp.where(mask_wide, w_master - learn_rate * adam_step, w_master)  22 us
    dot_general x1, matrix products, shards(): jnp.einsum('cjk,kcab->cjab', owner_map, new_tiles, precision=lax.Precisio...  11.6 us
  transfers between devices with their start and end apart: 6, of which 6 were waited for; matrix products, arithmetic and copies ran while one was open for 24% of the time, Pallas kernels for 0%

profile of v1, /device:TPU:13, one launch (start us, length us, event | category | flops | bytes accessed | tf_op | source)
XLA Modules:
  0.0 446.1 jit_solution(8407651596693543842)
XLA Ops:
  7.2 0.0 all-gather.4.cloned.1.call-start
  7.2 8.1 %all_gather.12 = bf16[512,512]{1,0:T(8,128)(2,1)S(1)} all-gather(bf16[256,512]{1,0:T(8,128)(2,1)} %param.7), channel_id=1, replica_groups=mesh['group'=2,'shard'=16] {'group'}, dimensions={0}, use_global_device_ids=true | all-gather | bytes 786432 | tf_op jit(solution)/shard_map/all_gather | solution.py:24
  15.3 0.8 compare_and_fusion
  16.0 1.2 gather_fusion
  17.2 0.8 broadcast_select_fusion
  18.0 0.0 all-gather.6.cloned.1.call-start
  18.1 7.3 %copy.16 = bf16[4096,512]{0,1:T(8,128)(2,1)} copy(f32[4096,512]{1,0:T(8,128)} %param.10) | data formatting | bytes 12582912 | tf_op args[3]
  25.4 0.0 reduce-scatter.2.cloned.1.call-start
  25.4 45.0 %all-gather.4.cloned.1.call-done = bf16[256,8192]{1,0:T(8,128)(2,1)} async-done(((bf16[256,512]{1,0:T(8,128)(2,1)}), bf16[256,8192]{1,0:T(8,128)(2,1)}) %all-gather.4.cloned.1.call-update) | async-done | bytes 4194320 | tf_op jit(solution)/shard_map/all_gather | solution.py:30
  70.4 8.0 %convolution_convert_fusion = bf16[8192,512]{1,0:T(8,128)(2,1)} fusion(bf16[256,8192]{1,0:T(8,128)(2,1)} %all-gather.4.cloned.1.call-done, bf16[256,512]{1,0:T(8,128)(2,1)S(1)} %copy-done), kind=kOutput, calls=%fused_computation.3 | convolution fusion | flops 2151677952 | bytes 12845056 | tf_op jit(solution)/shard_map/dot_general | solution.py:50
  78.4 98.4 %all-gather.6.cloned.1.call-done = bf16[8192,512]{0,1:T(8,128)(2,1)} async-done(((bf16[4096,512]{0,1:T(8,128)(2,1)}), bf16[8192,512]{0,1:T(8,128)(2,1)}) %all-gather.6.cloned.1.call-update) | async-done | bytes 8388624 | tf_op jit(solution)/shard_map/all_gather | solution.py:25
  176.8 1.9 fusion.26
  178.7 1.9 fusion.25
  180.5 1.9 fusion.24
  182.4 1.9 fusion.23
  184.3 1.9 fusion.22
  186.1 2.0 fusion.21
  188.2 1.9 fusion.20
  190.0 1.9 fusion.19
  191.9 1.9 fusion.18
  193.8 1.9 fusion.17
  195.7 1.9 fusion.16
  197.6 1.9 fusion.15
  199.5 1.9 fusion.14
  201.4 1.9 fusion.13
  203.3 1.8 fusion.12
  205.1 2.0 fusion.11
  207.1 6.5 %all-to-all-start = ((bf16[16,512,512]{1,2,0:T(8,128)(2,1)}), bf16[16,512,512]{1,2,0:T(8,128)(2,1)}, u32[]{:S(2)}, u32[]{:S(2)}) async-start(bf16[16,512,512]{1,2,0:T(8,128)(2,1)} %fusion.11), calls=%async_computation | async-start | bytes 16777216 | tf_op jit(solution)/shard_map/all_to_all | solution.py:36
  213.5 0.0 all-gather.8.cloned.1.call-start
  213.6 0.5 all-gather.8.cloned.1.call-update
  214.1 0.2 all-reduce.2.cloned.1.call-start
  214.4 0.1 dynamic-slice_reduce_fusion
  214.5 1.0 sort.17
  215.5 0.1 copy.17
  215.6 0.1 dynamic-slice_compare_fusion
  215.7 0.1 iota_compare_fusion
  215.7 8.0 %convolution_convert_fusion.2 = bf16[256,512]{1,0:T(8,128)(2,1)} fusion(bf16[256,8192]{1,0:T(8,128)(2,1)} %all-gather.4.cloned.1.call-done, bf16[8192,512]{0,1:T(8,128)(2,1)} %all-gather.6.cloned.1.call-done), kind=kOutput, calls=%fused_computation.14 | convolution fusion | flops 2147614720 | bytes 12845056 | tf_op jit(solution)/shard_map/dot_general | solution.py:33
  223.7 55.3 %reduce-scatter.2.cloned.1.call-done = bf16[4096,512]{1,0:T(8,128)(2,1)} async-done(((bf16[8192,512]{1,0:T(8,128)(2,1)}), bf16[4096,512]{1,0:T(8,128)(2,1)}) %reduce-scatter.2.cloned.1.call-update) | async-done | bytes 4194320 | tf_op jit(solution)/shard_map/reduce_scatter | solution.py:53
  279.0 1.1 broadcast_in_dim.26
  280.2 22.0 %subtract_select_fusion = (f32[4096,512]{1,0:T(8,128)}, f32[4096,512]{1,0:T(8,128)}, f32[4096,512]{1,0:T(8,128)}) fusion(f32[4096,512]{1,0:T(8,128)} %param.10, pred[512,8,4,128]{3,2,1,0:T(4,128)(4,1)S(1)} %bitcast.95, f32[4096,512]{1,0:T(8,128)} %param.11, bf16[4096,512]{1,0:T(8,128)(2,1)} %reduce-scatter.2.cloned.1.call-done, f32[4096,512]{1,0:T(8,128)} %param.12), kind=kLoop, calls=%fused_computation.1 | loop fusion | flops 35651584 | bytes 56623104 | tf_op jit(solution)/shard_map/jit(_where)/select_n | solution.py:70
  302.1 9.9 %reshape.59 = f32[32,128,4,128]{3,2,1,0:T(4,128)} reshape(f32[4096,512]{1,0:T(8,128)} %get-tuple-element.20) | data formatting | bytes 16777216 | tf_op jit(solution)/shard_map/reshape | solution.py:71
  312.1 11.6 %fusion.7 = bf16[4,6,128,128]{3,1,2,0:T(8,128)(2,1)} fusion(f32[32,128,4,128]{3,2,1,0:T(4,128)} %reshape.59, s32[32]{0:T(128)S(1)} %iota_add_fusion, s32[4,6]{1,0:T(4,128)S(1)} %copy.17, pred[4,6]{1,0:T(4,128)(4,1)S(1)} %iota_compare_fusion), kind=kOutput, calls=%fused_computation.12 | convolution fusion | flops 151389696 | bytes 9175288 | tf_op jit(solution)/shard_map/cjk,kcab->cjab/dot_general | solution.py:72
  323.7 70.7 %all-gather.8.cloned.1.call-done = bf16[256,8192]{1,0:T(8,128)(2,1)} async-done(((bf16[256,512]{1,0:T(8,128)(2,1)}), bf16[256,8192]{1,0:T(8,128)(2,1)}) %all-gather.8.cloned.1.call-update) | async-done | bytes 4194320 | tf_op jit(solution)/shard_map/all_gather | solution.py:31
  394.3 26.9 %all-to-all-done = bf16[16,512,512]{1,2,0:T(8,128)(2,1)} async-done(((bf16[16,512,512]{1,2,0:T(8,128)(2,1)}), bf16[16,512,512]{1,2,0:T(8,128)(2,1)}, u32[]{:S(2)}, u32[]{:S(2)}) %all-to-all-start) | async-done | bytes 8388640 | tf_op jit(solution)/shard_map/all_to_all | solution.py:36
  421.2 7.3 %fusion.10 = bf16[256,512]{0,1:T(8,128)(2,1)S(1)} fusion(bf16[512,8192]{0,1:T(8,128)(2,1)} %bitcast.17, bf16[256,8192]{1,0:T(8,128)(2,1)} %all-gather.8.cloned.1.call-done), kind=kOutput, calls=%fused_computation.15 | convolution fusion | flops 2147614720 | bytes 12845056 | tf_op jit(solution)/shard_map/dot_general | solution.py:38
  428.6 0.8 copy.19
  429.4 7.9 %all-reduce.2.cloned.1.call-done = bf16[4,6,128,128]{3,1,2,0:T(8,128)(2,1)} async-done(((bf16[4,6,128,128]{3,1,2,0:T(8,128)(2,1)}), bf16[4,6,128,128]{3,1,2,0:T(8,128)(2,1)}) %all-reduce.2.cloned.1.call-update) | async-done | bytes 786448 | tf_op jit(solution)/shard_map/psum | solution.py:75
  437.3 2.3 copy.20
  (12 shorter events, 0.1 us)
Async XLA Ops:
  7.2 63.3 %all-gather.4.cloned.1.call-start = ((), (), s32[]{:S(2)}) async-start(), calls=%async_computation.2 | async-start | bytes 4456448 | tf_op jit(solution)/shard_map/all_gather | solution.py:30
  18.0 52.4 %copy-start = (bf16[256,512]{1,0:T(8,128)(2,1)S(1)}, bf16[256,512]{1,0:T(8,128)(2,1)}, u32[]{:S(2)}) copy-start(bf16[256,512]{1,0:T(8,128)(2,1)} %param.9) | copy-start | bytes 786436
  18.0 158.7 %all-gather.6.cloned.1.call-start = ((), (), s32[]{:S(2)}) async-start(), calls=%async_computation.3 | async-start | bytes 12582912 | tf_op jit(solution)/shard_map/all_gather | solution.py:25
  25.4 253.6 %reduce-scatter.2.cloned.1.call-start = ((), (), s32[]{:S(2)}) async-start(), calls=%async_computation.5 | async-start | bytes 12582912 | tf_op jit(solution)/shard_map/reduce_scatter | solution.py:53
  207.1 7.3 %copy-start.1 = (s32[64,64]{1,0:T(8,128)S(1)}, s32[64,64]{1,0:T(8,128)}, u32[]{:S(2)}) copy-start(s32[64,64]{1,0:T(8,128)} %param.13) | copy-start | bytes 49156
  207.1 214.2 %all-to-all-start = ((bf16[16,512,512]{1,2,0:T(8,128)(2,1)}), bf16[16,512,512]{1,2,0:T(8,128)(2,1)}, u32[]{:S(2)}, u32[]{:S(2)}) async-start(bf16[16,512,512]{1,2,0:T(8,128)(2,1)} %fusion.11), calls=%async_computation | async-start | bytes 16777216 | tf_op jit(solution)/shard_map/all_to_all | solution.py:36
  213.5 180.8 %all-gather.8.cloned.1.call-start = ((), (), s32[]{:S(2)}) async-start(), calls=%async_computation.4 | async-start | bytes 4456448 | tf_op jit(solution)/shard_map/all_gather | solution.py:31
  214.1 223.2 %all-reduce.2.cloned.1.call-start = ((), (), s32[]{:S(2)}) async-start(), calls=%async_computation.6 | async-start | bytes 2097152 | tf_op jit(solution)/shard_map/psum | solution.py:75
Sparse Core Ops, SparseCore 0:
  18.2 52.2 all-gather.3
  72.5 104.1 all-gather.5
  179.7 99.3 reduce-scatter.1
  281.0 113.2 all-gather.7
  396.5 40.8 all-reduce.1
